TPU v7x, 32 devices: a whole 2x2x4 slice. The times are simulated.
32 devices in a mesh: grp: 1, col: 32 (over z, y, x, core).
Axes of the slice: x: 2, y: 2, z: 4, core: 2. Of those that a mesh axis runs over, the one named last changes fastest.
Arguments:
- pair: bfloat16 [16, 1024, 128], P('grp', 'col'), may hold values from -6 to 6
- w_query: bfloat16 [128, 128], replicated, may hold values from -0.5 to 0.5
- w_kv: bfloat16 [128, 256], replicated, may hold values from -0.5 to 0.5
- w_gate: bfloat16 [128, 128], replicated, may hold values from -0.5 to 0.5
- w_out: bfloat16 [128, 128], replicated, may hold values from -0.5 to 0.5
- pair_bias: bfloat16 [4, 1024, 1024], P('grp', 'col'), may hold values from -8 to 300
- lengths: int32 [1], P('grp'), may hold values from 512 to 1024
Outputs:
- update: bfloat16 [16, 1024, 128], P('grp', 'col')
All inputs are finite; a program needn't handle non-finite values.
Results may differ from a plain program's by a relative error of at most 0.0081.
Values may be sent and summed in bfloat16 or wider, within the bound.
No kernel may reach another device: no remote copies, remote signals or barrier semaphores. Data moves between devices by JAX's collectives and lax.ppermute only.
A program may use at most 128 MiB of HBM per device.

v0:
```python
import jax
import jax.numpy as jnp
from jax import lax
from jax.sharding import PartitionSpec as P

HEADS = 4


def normalize(pair_block):
    values_f = pair_block.astype(jnp.float32)
    mean_val = jnp.mean(values_f, axis=-1, keepdims=True)
    centred = values_f - mean_val
    variance = jnp.mean(centred * centred, axis=-1, keepdims=True)
    return (centred * lax.rsqrt(variance + 1e-05)).astype(jnp.bfloat16)


def attend(normed, bias_query, key_limit, w_query, w_kv, w_gate, w_out, gather_keys):
    row_count, col_count, chan_count = normed.shape
    head_width = chan_count // HEADS
    queries = (
        jnp.dot(normed, w_query, preferred_element_type=jnp.float32) * head_width ** (-0.5)
    ).astype(jnp.bfloat16)
    queries = queries.reshape(row_count, col_count, HEADS, head_width)
    gate_act = jax.nn.sigmoid(jnp.dot(normed, w_gate, preferred_element_type=jnp.float32))

    def consume(running, segment, offset):
        run_max, run_sum, run_acc = running
        key_value = jnp.dot(segment, w_kv, preferred_element_type=jnp.float32).astype(jnp.bfloat16)
        tile_len = key_value.shape[1]
        key_tile = key_value[:, :, :chan_count].reshape(row_count, tile_len, HEADS, head_width)
        value_tile = key_value[:, :, chan_count:].reshape(row_count, tile_len, HEADS, head_width)
        scores = jnp.einsum(
            "rjhd,rkhd->rhjk", queries, key_tile, preferred_element_type=jnp.float32
        )
        bias_part = lax.dynamic_slice_in_dim(bias_query, offset, tile_len, 2).astype(jnp.float32)
        key_pos = offset + jnp.arange(tile_len, dtype=jnp.int32)
        key_mask = jnp.where(key_pos < key_limit, 0.0, -1000000000.0).astype(jnp.float32)
        scores = scores + bias_part[None] + key_mask
        new_max = jnp.maximum(run_max, jnp.max(scores, axis=-1))
        rescale = jnp.exp(run_max - new_max)
        expon = jnp.exp(scores - new_max[..., None])
        new_sum = run_sum * rescale + jnp.sum(expon, axis=-1)
        weights = expon.astype(jnp.bfloat16)
        partial_out = jnp.einsum(
            "rhjk,rkhd->rjhd", weights, value_tile, preferred_element_type=jnp.float32
        )
        new_acc = run_acc * jnp.transpose(rescale, (0, 2, 1))[..., None] + partial_out
        return (new_max, new_sum, new_acc)

    def fold_piece(running, segment, offset, project):
        tile_len = segment.shape[1]
        block_len = 512
        block_num = tile_len // block_len
        blocks = jnp.moveaxis(
            segment.reshape(row_count, block_num, block_len, segment.shape[2]), 1, 0
        )

        def advance(state_now, item_pair):
            block_tile, block_idx = item_pair
            return (consume(state_now, block_tile, block_idx * block_len), None)

        final_state, unused = lax.scan(
            advance, running, (blocks, jnp.arange(block_num, dtype=jnp.int32))
        )
        return final_state

    initial = (
        jnp.full((row_count, HEADS, col_count), -1e30, jnp.float32),
        jnp.zeros((row_count, HEADS, col_count), jnp.float32),
        jnp.zeros((row_count, col_count, HEADS, head_width), jnp.float32),
    )
    run_max, run_sum, run_acc = gather_keys(fold_piece, initial)
    attended = run_acc / jnp.transpose(run_sum, (0, 2, 1))[..., None]
    hidden = (gate_act * attended.reshape(row_count, col_count, chan_count)).astype(jnp.bfloat16)
    return jnp.dot(hidden, w_out, preferred_element_type=jnp.float32).astype(jnp.bfloat16)


def on_device(pair, w_query, w_kv, w_gate, w_out, pair_bias, lengths):
    key_limit = lengths[0]
    normed = normalize(pair)
    received = lax.all_to_all(pair_bias, "col", split_axis=2, concat_axis=1, tiled=True)
    bias_query = jnp.transpose(received, (0, 2, 1))

    def gather_keys(fold_piece, initial):
        return fold_piece(
            initial, lax.all_gather(normed, "col", axis=1, tiled=True), jnp.int32(0), True
        )

    return attend(normed, bias_query, key_limit, w_query, w_kv, w_gate, w_out, gather_keys)


def solution(mesh):
    in_specs = (P("grp", "col", None), P(), P(), P(), P(), P("grp", "col", None), P("grp"))
    out_specs = P("grp", "col", None)
    return jax.shard_map(
        on_device, mesh=mesh, in_specs=in_specs, out_specs=out_specs, check_vma=False
    )
```

profile of v0, /device:TPU:0, one launch (start us, length us, event | category | flops | bytes accessed | tf_op | source)
XLA Modules:
  0.0 114.1 jit_solution(4545162258831155141)
XLA Ops:
  6.5 1.1 convert_reduce_fusion
  7.6 1.2 %fusion.30 = f32[16,32]{1,0:T(8,128)S(1)} fusion(bf16[16,32,128]{2,1,0:T(8,128)(2,1)} %param.9, f32[16,32]{1,0:T(8,128)S(1)} %broadcast_multiply_fusion), kind=kLoop, calls=%fused_computation.40 | loop fusion | flops 261632 | bytes 135168 | tf_op jit(solution)/shard_map/reduce_sum | solution.py:13
  8.8 1.8 %fusion.31 = bf16[16,32,128]{2,1,0:T(8,128)(2,1)} fusion(bf16[16,32,128]{2,1,0:T(8,128)(2,1)} %param.9, f32[16,32]{1,0:T(8,128)S(1)} %add_rsqrt_fusion, f32[16,32]{1,0:T(8,128)S(1)} %broadcast_multiply_fusion), kind=kLoop, calls=%fused_computation.41 | loop fusion | flops 262144 | bytes 266240 | tf_op jit(solution)/shard_map/convert_element_type | solution.py:14
  10.6 1.6 %copy.17 = bf16[4,32,1024]{1,0,2:T(4,128)(2,1)S(1)} copy(bf16[4,32,1024]{2,1,0:T(8,128)(2,1)} %param.14) | data formatting | bytes 524288 | tf_op args[5]
  12.2 1.7 %reshape.48 = bf16[32,2,2048]{2,1,0:T(2,128)(2,1)} reshape(bf16[1024,4,32]{2,1,0:T(4,128)(2,1)S(1)} %bitcast.92) | data formatting | bytes 524288
  13.9 7.3 %all-to-all-start = ((bf16[32,2,2048]{2,1,0:T(2,128)(2,1)}), bf16[32,2,2048]{2,1,0:T(2,128)(2,1)S(1)}, u32[]{:S(2)}, u32[]{:S(2)}) async-start(bf16[32,2,2048]{2,1,0:T(2,128)(2,1)} %reshape.48), calls=%async_computation | async-start | bytes 524288 | tf_op jit(solution)/shard_map/all_to_all | solution.py:81
  21.3 1.1 fusion.27
  22.6 0.9 copy.21
  23.5 0.7 copy.20
  24.3 8.9 %all-to-all-done = bf16[32,2,2048]{2,1,0:T(2,128)(2,1)S(1)} async-done(((bf16[32,2,2048]{2,1,0:T(2,128)(2,1)}), bf16[32,2,2048]{2,1,0:T(2,128)(2,1)S(1)}, u32[]{:S(2)}, u32[]{:S(2)}) %all-to-all-start) | async-done | bytes 262176 | tf_op jit(solution)/shard_map/all_to_all | solution.py:81
  33.2 0.5 reshape.49
  33.7 0.7 copy.18
  34.4 1.1 all_to_all.16
  35.5 42.7 %all-gather.2.cloned.1.call-done = bf16[16,1024,128]{2,1,0:T(8,128)(2,1)} async-done(((bf16[16,32,128]{2,1,0:T(8,128)(2,1)}), bf16[16,1024,128]{2,1,0:T(8,128)(2,1)}) %all-gather.2.cloned.1.call-update) | async-done | bytes 4194320 | tf_op jit(solution)/shard_map/all_gather | solution.py:86
  78.2 26.6 %while.15 = (s32[]{:T(128)}, f32[16,4,32]{2,1,0:T(4,128)S(1)}, f32[16,4,32]{2,1,0:T(4,128)S(1)}, f32[16,32,4,32]{1,3,2,0:T(8,128)S(1)}, bf16[2,16,512,128]{3,2,0...) while((s32[]{:T(128)}, f32[16,4,32]{2,1,0:T(4,128)S(1)}, ...), condition=%wide.region_5.6_spmd.clone, body=%wide.region_2.5_spmd.clone.sunk | while | flops 684996096 | bytes 52896580 | solution.py:62
  78.2 0.6 dynamic_slice.24
  79.4 0.7 fusion.63
  80.1 2.9 %convolution_convert_fusion.3 = bf16[16,512,256]{1,2,0:T(8,128)(2,1)S(1)} fusion(bf16[2,16,512,128]{3,2,0,1:T(8,128)(2,1)} %get-tuple-element.254, s32[]{:T(128)} %get-tuple-element.236, bf16[128,256]{0,1:T(8,128)(2,1)} %get-tuple-element.255), kind=kOutput, calls=%fused_computation.6.clone.1 | convolution fusion | flops 538968064 | bytes 6357504 | tf_op jit(solution)/shard_map/while/body/eval_jaxpr/dot_general | solution.py:28
  83.0 0.3 fusion.64
  83.3 0.7 copy-done.2
  84.0 2.7 %fusion.65 = (f32[16,4,32]{2,1,0:T(4,128)S(1)}, f32[16,4,512,32]{2,3,1,0:T(8,128)}) fusion(f32[512]{0:T(512)S(1)} %fusion.63, f32[4,32,512]{2,1,0:T(8,128)S(1)} %dynamic-slice_convert_fusion.2, bf16[16,32,4,32]{3,1,2,0:T(8,128)(2,1)S(1)} %copy-done.2, bf16[16,512,4,32]{1,3,2,0:T(8,128)(2,1)S(1)} %bitcast.90), kind=kOutput, calls=%fused_computation.5.clone.1 | convolution fusion | flops 70252544 | bytes 6694912 | tf_op jit(solution)/shard_map/while/body/eval_jaxpr/rjhd,rkhd->rhjk/dot_general | solution.py:32
  86.8 3.4 %fusion.69 = f32[16,32,4,32]{1,3,2,0:T(8,128)S(1)} fusion(bf16[16,512,4,32]{1,3,2,0:T(8,128)(2,1)S(1)} %bitcast.89, f32[16,4,512,32]{2,3,1,0:T(8,128)} %get-tuple-element.219, f32[16,4,32]{2,1,0:T(4,128)S(1)} %get-tuple-element.251, f32[512]{0:T(512)S(1)} %fusion.63, f32[4,32,512]{2,1,0:T(8,128)S(1)} %dynamic-slice_convert_fusion.2, ...), kind=kOutput, calls=%fused_computation.14.clone.1 | convolution fusion | flops 71499776 | bytes 7096321 | tf_op jit(solution)/shard_map/while/body/eval_jaxpr/rhjk,rkhd->rjhd/dot_general | solution.py:44
  90.2 1.2 %fusion.67 = f32[16,4,32]{2,1,0:T(4,128)S(1)} fusion(f32[16,4,512,32]{2,3,1,0:T(8,128)S(1)} %copy-done.1, f32[16,4,32]{2,1,0:T(4,128)S(1)} %get-tuple-element.251, f32[512]{0:T(512)S(1)} %fusion.63, f32[4,32,512]{2,1,0:T(8,128)S(1)} %dynamic-slice_convert_fusion.2), kind=kLoop, calls=%fused_computation.4.clone.1 | loop fusion | flops 4192256 | bytes 4474880 | tf_op jit(solution)/shard_map/while/body/eval_jaxpr/reduce_sum | solution.py:42
  91.5 0.6 dynamic_slice.24
  92.7 0.7 fusion.63
  93.4 2.9 %convolution_convert_fusion.3 = bf16[16,512,256]{1,2,0:T(8,128)(2,1)S(1)} fusion(bf16[2,16,512,128]{3,2,0,1:T(8,128)(2,1)} %get-tuple-element.254, s32[]{:T(128)} %get-tuple-element.236, bf16[128,256]{0,1:T(8,128)(2,1)} %get-tuple-element.255), kind=kOutput, calls=%fused_computation.6.clone.1 | convolution fusion | flops 538968064 | bytes 6357504 | tf_op jit(solution)/shard_map/while/body/eval_jaxpr/dot_general | solution.py:28
  96.2 0.3 fusion.64
  96.6 0.7 copy-done.2
  97.3 2.8 %fusion.65 = (f32[16,4,32]{2,1,0:T(4,128)S(1)}, f32[16,4,512,32]{2,3,1,0:T(8,128)}) fusion(f32[512]{0:T(512)S(1)} %fusion.63, f32[4,32,512]{2,1,0:T(8,128)S(1)} %dynamic-slice_convert_fusion.2, bf16[16,32,4,32]{3,1,2,0:T(8,128)(2,1)S(1)} %copy-done.2, bf16[16,512,4,32]{1,3,2,0:T(8,128)(2,1)S(1)} %bitcast.90), kind=kOutput, calls=%fused_computation.5.clone.1 | convolution fusion | flops 70252544 | bytes 6694912 | tf_op jit(solution)/shard_map/while/body/eval_jaxpr/rjhd,rkhd->rhjk/dot_general | solution.py:32
  100.1 3.4 %fusion.69 = f32[16,32,4,32]{1,3,2,0:T(8,128)S(1)} fusion(bf16[16,512,4,32]{1,3,2,0:T(8,128)(2,1)S(1)} %bitcast.89, f32[16,4,512,32]{2,3,1,0:T(8,128)} %get-tuple-element.219, f32[16,4,32]{2,1,0:T(4,128)S(1)} %get-tuple-element.251, f32[512]{0:T(512)S(1)} %fusion.63, f32[4,32,512]{2,1,0:T(8,128)S(1)} %dynamic-slice_convert_fusion.2, ...), kind=kOutput, calls=%fused_computation.14.clone.1 | convolution fusion | flops 71499776 | bytes 7096321 | tf_op jit(solution)/shard_map/while/body/eval_jaxpr/rhjk,rkhd->rjhd/dot_general | solution.py:44
  103.5 1.2 %fusion.67 = f32[16,4,32]{2,1,0:T(4,128)S(1)} fusion(f32[16,4,512,32]{2,3,1,0:T(8,128)S(1)} %copy-done.1, f32[16,4,32]{2,1,0:T(4,128)S(1)} %get-tuple-element.251, f32[512]{0:T(512)S(1)} %fusion.63, f32[4,32,512]{2,1,0:T(8,128)S(1)} %dynamic-slice_convert_fusion.2), kind=kLoop, calls=%fused_computation.4.clone.1 | loop fusion | flops 4192256 | bytes 4474880 | tf_op jit(solution)/shard_map/while/body/eval_jaxpr/reduce_sum | solution.py:42
  105.3 1.9 %convolution_convert_fusion.1 = bf16[16,32,128]{2,1,0:T(8,128)(2,1)} fusion(f32[16,32,128]{2,1,0:T(8,128)S(1)} %copy.23, bf16[16,32,128]{2,1,0:T(8,128)(2,1)} %fusion.31, bf16[128,128]{1,0:T(8,128)(2,1)} %param.13, bf16[128,128]{1,0:T(8,128)(2,1)} %param.12), kind=kOutput, calls=%fused_computation.34 | convolution fusion | flops 33947648 | bytes 589824 | tf_op jit(solution)/shard_map/dot_general | solution.py:75
  (37 shorter events, 1.0 us)
Async XLA Ops:
  6.5 14.7 %copy-start = (bf16[128,128]{1,0:T(8,128)(2,1)S(1)}, bf16[128,128]{1,0:T(8,128)(2,1)}, u32[]{:S(2)}) copy-start(bf16[128,128]{1,0:T(8,128)(2,1)} %param.10) | copy-start | bytes 98308
  6.5 17.0 %copy-start.5 = (bf16[128,256]{1,0:T(8,128)(2,1)S(1)}, bf16[128,256]{1,0:T(8,128)(2,1)}, u32[]{:S(2)}) copy-start(bf16[128,256]{1,0:T(8,128)(2,1)} %param.11) | copy-start | bytes 196612
  6.5 71.7 %all-gather.2.cloned.1.call-start = ((), (), s32[]{:S(2)}) async-start(), calls=%async_computation.1 | async-start | bytes 4325376 | tf_op jit(solution)/shard_map/all_gather | solution.py:86
  13.9 19.3 %all-to-all-start = ((bf16[32,2,2048]{2,1,0:T(2,128)(2,1)}), bf16[32,2,2048]{2,1,0:T(2,128)(2,1)S(1)}, u32[]{:S(2)}, u32[]{:S(2)}) async-start(bf16[32,2,2048]{2,1,0:T(2,128)(2,1)} %reshape.48), calls=%async_computation | async-start | bytes 524288 | tf_op jit(solution)/shard_map/all_to_all | solution.py:81
  78.2 1.9 %copy-start.3 = (bf16[4,32,1024]{2,1,0:T(8,128)(2,1)}, bf16[4,32,1024]{2,1,0:T(8,128)(2,1)S(1)}, u32[]{:S(2)}) copy-start(bf16[4,32,1024]{2,1,0:T(8,128)(2,1)S(1)} %get-tuple-element.258) | copy-start | bytes 786436 | tf_op jit(solution)/shard_map/while
  82.9 1.0 copy-start.2
  86.8 3.5 %copy-start.1 = (f32[16,4,512,32]{2,3,1,0:T(8,128)S(1)}, f32[16,4,512,32]{2,3,1,0:T(8,128)}, u32[]{:S(2)}) copy-start(f32[16,4,512,32]{2,3,1,0:T(8,128)} %get-tuple-element.219) | copy-start | bytes 12582916 | tf_op jit(solution)/shard_map/while
  90.2 1.3 %copy-start.4 = (bf16[4,32,1024]{2,1,0:T(8,128)(2,1)S(1)}, bf16[4,32,1024]{2,1,0:T(8,128)(2,1)}, u32[]{:S(2)}) copy-start(bf16[4,32,1024]{2,1,0:T(8,128)(2,1)} %copy-done.3) | copy-start | bytes 786436 | tf_op jit(solution)/shard_map/while
  91.5 1.9 %copy-start.3 = (bf16[4,32,1024]{2,1,0:T(8,128)(2,1)}, bf16[4,32,1024]{2,1,0:T(8,128)(2,1)S(1)}, u32[]{:S(2)}) copy-start(bf16[4,32,1024]{2,1,0:T(8,128)(2,1)S(1)} %get-tuple-element.258) | copy-start | bytes 786436 | tf_op jit(solution)/shard_map/while
  96.2 1.0 copy-start.2
  100.1 3.5 %copy-start.1 = (f32[16,4,512,32]{2,3,1,0:T(8,128)S(1)}, f32[16,4,512,32]{2,3,1,0:T(8,128)}, u32[]{:S(2)}) copy-start(f32[16,4,512,32]{2,3,1,0:T(8,128)} %get-tuple-element.219) | copy-start | bytes 12582916 | tf_op jit(solution)/shard_map/while
  103.5 1.3 %copy-start.4 = (bf16[4,32,1024]{2,1,0:T(8,128)(2,1)S(1)}, bf16[4,32,1024]{2,1,0:T(8,128)(2,1)}, u32[]{:S(2)}) copy-start(bf16[4,32,1024]{2,1,0:T(8,128)(2,1)} %copy-done.3) | copy-start | bytes 786436 | tf_op jit(solution)/shard_map/while
Sparse Core Ops, SparseCore 0:
  10.7 67.4 all-gather.1
where the time goes:
time: 115 us; the launch traced here: 114 us
  waiting for transfers between devices  51.7 us (45%)
  matrix products  21.1 us (18%)
  between operations  13.5 us (12%)
  local copies, waits for them, and re-layouts  11.1 us (10%)
  other arithmetic  8.07 us (7%)
  starting transfers between devices  7.33 us (6%)
  loops' own time  1.32 us (1%)
    all_gather x1, waiting for transfers between devices, gather_keys(): lax.all_gather(normed, 'col', axis=1, tiled=True)  42.7 us
    all_to_all x1, waiting for transfers between devices, on_device(): lax.all_to_all(pair_bias, 'col', split_axis=2, concat_axis=1, tiled=True)  8.93 us
    all_to_all x1, starting transfers between devices, on_device(): lax.all_to_all(pair_bias, 'col', split_axis=2, concat_axis=1, tiled=True)  7.33 us
    dot_general x2, matrix products, consume(): jnp.einsum('rhjk,rkhd->rjhd', weights, value_tile, preferred_element_type...  6.85 us
    dot_general x2, matrix products, consume(): jnp.dot(segment, w_kv, preferred_element_type=jnp.float32)  5.72 us
    dot_general x2, matrix products, consume(): jnp.einsum('rjhd,rkhd->rhjk', queries, key_tile, preferred_element_type=j...  5.51 us
    unnamed x9, local copies, waits for them, and re-layouts  5.47 us
    reduce_sum x2, other arithmetic, consume(): new_sum = run_sum * rescale + jnp.sum(expon, axis=-1)  2.38 us
  transfers between devices with their start and end apart: 2, of which 2 were waited for; matrix products, arithmetic and copies ran while one was open for 7% of the time, Pallas kernels for 0%

commit v1 on v0

--- a/solution.py
+++ b/solution.py
@@ -4,6 +4,28 @@
 from jax.sharding import PartitionSpec as P
 
 HEADS = 4
+
+
+def joined_along(pieces, dim):
+    lengths = list(pieces.shape[1:])
+    lengths[dim] *= pieces.shape[0]
+    return jnp.moveaxis(pieces, 0, dim).reshape(lengths)
+
+
+def collected_by_bits(shard, axis):
+    size = lax.axis_size(axis)
+    blocks = shard[None]
+    for level in range(size.bit_length() - 1):
+        stride = 1 << level
+        other = lax.ppermute(blocks, axis, [(i, i ^ stride) for i in range(size)])
+        both = jnp.stack([blocks, other])
+        upper = lax.axis_index(axis) >> level & 1
+        blocks = jnp.where(upper == 0, both, both[::-1]).reshape(-1, *shard.shape)
+    return blocks
+
+
+def collect(value, axis, dim):
+    return joined_along(collected_by_bits(value, axis), dim)
 
 
 def normalize(pair_block):
@@ -82,9 +104,7 @@
     bias_query = jnp.transpose(received, (0, 2, 1))
 
     def gather_keys(fold_piece, initial):
-        return fold_piece(
-            initial, lax.all_gather(normed, "col", axis=1, tiled=True), jnp.int32(0), True
-        )
+        return fold_piece(initial, collect(normed, "col", 1), jnp.int32(0), True)
 
     return attend(normed, bias_query, key_limit, w_query, w_kv, w_gate, w_out, gather_keys)
 

time: 115 us -> 195 us (1.70)
  waiting for transfers between devices: 51.7 us -> 125 us
  between operations: 13.5 us -> 0.23 us
  local copies, waits for them, and re-layouts: 11.1 us -> 20 us
  other arithmetic: 8.07 us -> 14.6 us
  starting transfers between devices: 7.33 us -> 13.4 us
    all_to_all x1, waiting for transfers between devices: 8.93 us -> 83.1 us  [on_device(): lax.all_to_all(pair_bias, 'col', split_axis=2, concat_axis=1, tiled=True)]
    all_gather x1 -> x0, waiting for transfers between devices: 42.7 us -> none  [gather_keys(): lax.all_gather(normed, 'col', axis=1, tiled=True)]
    ppermute x0 -> x5, waiting for transfers between devices: none -> 41.5 us  [collected_by_bits(): other = lax.ppermute(blocks, axis, [(i, i ^ stride) for i in range(size)])]
    ppermute x0 -> x5, starting transfers between devices: none -> 9.25 us  [collected_by_bits(): other = lax.ppermute(blocks, axis, [(i, i ^ stride) for i in range(size)])]
    select_n x0 -> x4, other arithmetic: none -> 4.41 us  [collected_by_bits(): blocks = jnp.where(upper == 0, both, both[::-1]).reshape(-1, *shard.shape)]
    unnamed x9 -> x13, local copies, waits for them, and re-layouts: 5.47 us -> 9.85 us
    another operation x0 -> x7, other arithmetic: none -> 3.91 us  [collected_by_bits(): both = jnp.stack([blocks, other])]
    all_to_all x2, local copies, waits for them, and re-layouts: 1.77 us -> 5.21 us  [on_device(): lax.all_to_all(pair_bias, 'col', split_axis=2, concat_axis=1, tiled=True)]
  transfers between devices with their start and end apart: 2 -> 6, of which waited for: 2 -> 5; matrix products, arithmetic and copies ran while one was open for 7% -> 7% of each run, Pallas kernels for 0% -> 0%
where the time goes in v1:
time: 195 us
  waiting for transfers between devices  125 us (64%)
  matrix products  20.4 us (10%)
  local copies, waits for them, and re-layouts  20 us (10%)
  other arithmetic  14.6 us (7%)
  starting transfers between devices  13.4 us (7%)
    all_to_all x1, waiting for transfers between devices, on_device(): lax.all_to_all(pair_bias, 'col', split_axis=2, concat_axis=1, tiled=True)  83.1 us
    ppermute x5, waiting for transfers between devices, collected_by_bits(): other = lax.ppermute(blocks, axis, [(i, i ^ stride) for i in range(size)])  41.5 us
    unnamed x13, local copies, waits for them, and re-layouts  9.85 us
    ppermute x5, starting transfers between devices, collected_by_bits(): other = lax.ppermute(blocks, axis, [(i, i ^ stride) for i in range(size)])  9.25 us
    dot_general x2, matrix products, consume(): jnp.einsum('rhjk,rkhd->rjhd', weights, value_tile, preferred_element_type...  6.86 us
    dot_general x2, matrix products, consume(): jnp.dot(segment, w_kv, preferred_element_type=jnp.float32)  5.71 us
    dot_general x2, matrix products, consume(): jnp.einsum('rjhd,rkhd->rhjk', queries, key_tile, preferred_element_type=j...  5.49 us
    all_to_all x2, local copies, waits for them, and re-layouts, on_device(): lax.all_to_all(pair_bias, 'col', split_axis=2, concat_axis=1, tiled=True)  5.21 us
  transfers between devices with their start and end apart: 6, of which 5 were waited for; matrix products, arithmetic and copies ran while one was open for 7% of the time, Pallas kernels for 0%

profile of v1, /device:TPU:0, one launch (start us, length us, event | category | flops | bytes accessed | tf_op | source)
XLA Modules:
  0.0 194.8 jit_solution(13374826686227610735)
XLA Ops:
  0.0 1.0 convert_reduce_fusion
  1.1 1.2 fusion.30
  2.3 1.1 fusion.41
  5.0 2.9 %collective-permute-start.1 = (bf16[2,16,32,128]{3,2,1,0:T(8,128)(2,1)S(1)}, bf16[2,16,32,128]{3,2,1,0:T(8,128)(2,1)S(1)}, u32[]{:S(2)}, u32[]{:S(2)}) collective-permute-start(bf16[2,16,32,128]{3,2,1,0:T(8,128)(2,1)S(1)} %get-tuple-element.150), channel_id=1, source_target_pairs={{0,2},{1,3},{2,0},{3,1},{4,6},{5,7},{6,4},{7,5},{8,10},{9,11},{10,... | collective-permute-start | bytes 786440 | tf_op jit(solution)/shard_map/ppermute | solution.py:20
  7.9 6.6 %collective-permute-done.1 = bf16[2,16,32,128]{3,2,1,0:T(8,128)(2,1)S(1)} collective-permute-done((bf16[2,16,32,128]{3,2,1,0:T(8,128)(2,1)S(1)}, bf16[2,16,32,128]{3,2,1,0:T(8,128)(2,1)S(1)}, u32[]{:S(2)}, u32[]{:S(2)}) %collective-permute-start.1) | collective-permute-done | bytes 262176 | tf_op jit(solution)/shard_map/ppermute | solution.py:20
  14.7 1.8 collective-permute-start.2
  16.6 11.6 %collective-permute-done.2 = bf16[4,16,32,128]{3,2,1,0:T(8,128)(2,1)S(1)} collective-permute-done((bf16[4,16,32,128]{3,2,1,0:T(8,128)(2,1)S(1)}, bf16[4,16,32,128]{3,2,1,0:T(8,128)(2,1)S(1)}, u32[]{:S(2)}, u32[]{:S(2)}) %collective-permute-start.2) | collective-permute-done | bytes 524320 | tf_op jit(solution)/shard_map/ppermute | solution.py:20
  28.6 1.6 collective-permute-start.3
  30.2 22.2 %collective-permute-done.3 = bf16[8,16,32,128]{3,2,0,1:T(8,128)(2,1)S(1)} collective-permute-done((bf16[8,16,32,128]{3,2,0,1:T(8,128)(2,1)S(1)}, bf16[8,16,32,128]{3,2,0,1:T(8,128)(2,1)S(1)}, u32[]{:S(2)}, u32[]{:S(2)}) %collective-permute-start.3) | collective-permute-done | bytes 1048608 | tf_op jit(solution)/shard_map/ppermute | solution.py:20
  53.8 2.3 %collective-permute-start.4 = (bf16[16,16,32,128]{3,2,0,1:T(8,128)(2,1)S(1)}, bf16[16,16,32,128]{3,2,0,1:T(8,128)(2,1)}, u32[]{:S(2)}, u32[]{:S(2)}) collective-permute-start(bf16[16,16,32,128]{3,2,0,1:T(8,128)(2,1)S(1)} %bitcast.121), channel_id=1, source_target_pairs={{0,16},{1,17},{2,18},{3,19},{4,20},{5,21},{6,22},{7,23},{8,24},{9,... | collective-permute-start | bytes 6291464 | tf_op jit(solution)/shard_map/ppermute | solution.py:20
  56.1 1.6 copy.21
  57.7 1.7 reshape.64
  59.4 4.1 %all-to-all-start = ((bf16[32,2,2048]{2,1,0:T(2,128)(2,1)}), bf16[32,2,2048]{2,1,0:T(2,128)(2,1)}, u32[]{:S(2)}, u32[]{:S(2)}) async-start(bf16[32,2,2048]{2,1,0:T(2,128)(2,1)} %reshape.64), calls=%async_computation | async-start | bytes 524288 | tf_op jit(solution)/shard_map/all_to_all | solution.py:103
  63.9 1.1 reshape.56
  65.0 2.0 %copy.25 = bf16[16,32,4,32]{3,1,2,0:T(8,128)(2,1)} copy(bf16[16,32,4,32]{3,2,1,0:T(4,128)(2,1)} %reshape.56) | data formatting | bytes 262144
  67.0 1.6 copy.24
  68.5 83.1 %all-to-all-done = bf16[32,2,2048]{2,1,0:T(2,128)(2,1)} async-done(((bf16[32,2,2048]{2,1,0:T(2,128)(2,1)}), bf16[32,2,2048]{2,1,0:T(2,128)(2,1)}, u32[]{:S(2)}, u32[]{:S(2)}) %all-to-all-start) | async-done | bytes 262176 | tf_op jit(solution)/shard_map/all_to_all | solution.py:103
  151.6 3.0 %reshape.65 = bf16[1024,4,32]{2,1,0:T(4,128)(2,1)} reshape(bf16[32,2,2048]{2,1,0:T(2,128)(2,1)} %all-to-all-done) | data formatting | bytes 524288
  154.6 2.9 %copy.22 = bf16[4,32,32,32]{2,1,3,0:T(8,128)(2,1)} copy(bf16[4,32,32,32]{2,0,3,1:T(4,128)(2,1)} %bitcast.125) | data formatting | bytes 524288 | tf_op jit(solution)/shard_map/all_to_all | solution.py:103
  157.5 2.3 %all_to_all.16 = bf16[4,1024,32]{1,2,0:T(8,128)(2,1)S(1)} reshape(bf16[4,32,32,32]{2,1,3,0:T(8,128)(2,1)} %copy.22) | data formatting | bytes 524288 | tf_op jit(solution)/shard_map/all_to_all | solution.py:103
  159.9 2.0 %pad_maximum_fusion = bf16[2,16,16,32,128]{4,3,1,0,2:T(8,128)(2,1)S(1)} fusion(bf16[1,16,16,32,128]{4,3,1,0,2:T(8,128)(2,1)} %bitcast.15, bf16[1,16,16,32,128]{4,3,1,0,2:T(8,128)(2,1)S(1)} %bitcast.122), kind=kLoop, calls=%fused_computation.27 | loop fusion | flops 2097152 | bytes 8388608 | tf_op jit(solution)/shard_map/stack | solution.py:21
  161.9 3.4 %reverse_select_fusion = bf16[2,16,16,32,128]{4,3,1,0,2:T(8,128)(2,1)} fusion(bf16[2,16,16,32,128]{4,3,1,0,2:T(8,128)(2,1)S(1)} %pad_maximum_fusion, pred[]{:T(512)S(6)} %eq.15), kind=kLoop, calls=%fused_computation.26 | loop fusion | flops 2097152 | bytes 8388609 | tf_op jit(solution)/shard_map/jit(_where)/select_n | solution.py:23
  165.3 27.0 %while.15 = (s32[]{:T(128)}, f32[16,4,32]{2,1,0:T(4,128)S(1)}, f32[16,4,32]{2,1,0:T(4,128)S(1)}, f32[16,32,4,32]{1,3,2,0:T(8,128)S(1)}, bf16[2,16,512,128]{3,2,0...) while((s32[]{:T(128)}, f32[16,4,32]{2,1,0:T(4,128)S(1)}, ...), condition=%wide.region_5.6_spmd.clone, body=%wide.region_2.5_spmd.clone.sunk | while | flops 684996096 | bytes 53158760 | solution.py:84
  167.3 2.9 %convolution_convert_fusion.3 = bf16[16,512,256]{1,2,0:T(8,128)(2,1)S(1)} fusion(bf16[2,16,512,128]{3,2,0,1:T(8,128)(2,1)} %get-tuple-element.258, s32[]{:T(128)} %get-tuple-element.240, bf16[128,256]{0,1:T(8,128)(2,1)S(1)} %get-tuple-element.259), kind=kOutput, calls=%fused_computation.6.clone.1 | convolution fusion | flops 538968064 | bytes 6357504 | tf_op jit(solution)/shard_map/while/body/eval_jaxpr/dot_general | solution.py:50
  171.2 2.7 %fusion.72 = (f32[16,4,32]{2,1,0:T(4,128)S(1)}, f32[16,4,512,32]{2,3,1,0:T(8,128)}) fusion(f32[512]{0:T(512)S(1)} %fusion.70, f32[4,32,512]{2,1,0:T(8,128)S(1)} %dynamic-slice_convert_fusion.2, bf16[16,32,4,32]{3,1,2,0:T(8,128)(2,1)S(1)} %copy-done.2, bf16[16,512,4,32]{1,3,2,0:T(8,128)(2,1)S(1)} %bitcast.117), kind=kOutput, calls=%fused_computation.5.clone.1 | convolution fusion | flops 70252544 | bytes 6694912 | tf_op jit(solution)/shard_map/while/body/eval_jaxpr/rjhd,rkhd->rhjk/dot_general | solution.py:54
  174.0 3.4 %fusion.76 = f32[16,32,4,32]{1,3,2,0:T(8,128)S(1)} fusion(bf16[16,512,4,32]{1,3,2,0:T(8,128)(2,1)S(1)} %bitcast.116, f32[16,4,512,32]{2,3,1,0:T(8,128)} %get-tuple-element.223, f32[16,4,32]{2,1,0:T(4,128)S(1)} %get-tuple-element.255, f32[512]{0:T(512)S(1)} %fusion.70, f32[4,32,512]{2,1,0:T(8,128)S(1)} %dynamic-slice_convert_fusion.2, ...), kind=kOutput, calls=%fused_computation.14.clone.1 | convolution fusion | flops 71499776 | bytes 7096321 | tf_op jit(solution)/shard_map/while/body/eval_jaxpr/rhjk,rkhd->rjhd/dot_general | solution.py:66
  177.5 1.2 fusion.74
  180.8 2.9 %convolution_convert_fusion.3 = bf16[16,512,256]{1,2,0:T(8,128)(2,1)S(1)} fusion(bf16[2,16,512,128]{3,2,0,1:T(8,128)(2,1)} %get-tuple-element.258, s32[]{:T(128)} %get-tuple-element.240, bf16[128,256]{0,1:T(8,128)(2,1)S(1)} %get-tuple-element.259), kind=kOutput, calls=%fused_computation.6.clone.1 | convolution fusion | flops 538968064 | bytes 6357504 | tf_op jit(solution)/shard_map/while/body/eval_jaxpr/dot_general | solution.py:50
  184.8 2.7 %fusion.72 = (f32[16,4,32]{2,1,0:T(4,128)S(1)}, f32[16,4,512,32]{2,3,1,0:T(8,128)}) fusion(f32[512]{0:T(512)S(1)} %fusion.70, f32[4,32,512]{2,1,0:T(8,128)S(1)} %dynamic-slice_convert_fusion.2, bf16[16,32,4,32]{3,1,2,0:T(8,128)(2,1)S(1)} %copy-done.2, bf16[16,512,4,32]{1,3,2,0:T(8,128)(2,1)S(1)} %bitcast.117), kind=kOutput, calls=%fused_computation.5.clone.1 | convolution fusion | flops 70252544 | bytes 6694912 | tf_op jit(solution)/shard_map/while/body/eval_jaxpr/rjhd,rkhd->rhjk/dot_general | solution.py:54
  187.5 3.4 %fusion.76 = f32[16,32,4,32]{1,3,2,0:T(8,128)S(1)} fusion(bf16[16,512,4,32]{1,3,2,0:T(8,128)(2,1)S(1)} %bitcast.116, f32[16,4,512,32]{2,3,1,0:T(8,128)} %get-tuple-element.223, f32[16,4,32]{2,1,0:T(4,128)S(1)} %get-tuple-element.255, f32[512]{0:T(512)S(1)} %fusion.70, f32[4,32,512]{2,1,0:T(8,128)S(1)} %dynamic-slice_convert_fusion.2, ...), kind=kOutput, calls=%fused_computation.14.clone.1 | convolution fusion | flops 71499776 | bytes 7096321 | tf_op jit(solution)/shard_map/while/body/eval_jaxpr/rhjk,rkhd->rjhd/dot_general | solution.py:66
  191.0 1.2 fusion.74
  192.8 2.0 %convolution_convert_fusion.1 = bf16[16,32,128]{2,1,0:T(8,128)(2,1)} fusion(f32[16,32,128]{2,1,0:T(8,128)S(1)} %copy.27, bf16[128,128]{1,0:T(8,128)(2,1)} %param.13, bf16[128,128]{1,0:T(8,128)(2,1)} %param.12, bf16[16,32,128]{2,1,0:T(8,128)(2,1)} %param.9, f32[16,32]{1,0:T(8,128)} %copy-done.8, f32[16,32]{1,0:T(8,128)S(1)} %broadcast_multiply_fusion), kind=kOutput, calls=%fused_computation.39 | convolution fusion | flops 34209792 | bytes 593920 | tf_op jit(solution)/shard_map/dot_general | solution.py:97
  (63 shorter events, 9.3 us)
Async XLA Ops:
  0.0 63.6 %copy-start = (bf16[128,128]{1,0:T(8,128)(2,1)S(1)}, bf16[128,128]{1,0:T(8,128)(2,1)}, u32[]{:S(2)}) copy-start(bf16[128,128]{1,0:T(8,128)(2,1)} %param.10) | copy-start | bytes 98308
  2.2 61.3 %copy-start.8 = (f32[16,32]{1,0:T(8,128)}, f32[16,32]{1,0:T(8,128)S(1)}, u32[]{:S(2)}) copy-start(f32[16,32]{1,0:T(8,128)S(1)} %add_rsqrt_fusion) | copy-start | bytes 6148
  3.4 1.5 collective-permute-start
  5.0 9.5 %collective-permute-start.1 = (bf16[2,16,32,128]{3,2,1,0:T(8,128)(2,1)S(1)}, bf16[2,16,32,128]{3,2,1,0:T(8,128)(2,1)S(1)}, u32[]{:S(2)}, u32[]{:S(2)}) collective-permute-start(bf16[2,16,32,128]{3,2,1,0:T(8,128)(2,1)S(1)} %get-tuple-element.150), channel_id=1, source_target_pairs={{0,2},{1,3},{2,0},{3,1},{4,6},{5,7},{6,4},{7,5},{8,10},{9,11},{10,... | collective-permute-start | bytes 786440 | tf_op jit(solution)/shard_map/ppermute | solution.py:20
  14.7 13.5 %collective-permute-start.2 = (bf16[4,16,32,128]{3,2,1,0:T(8,128)(2,1)S(1)}, bf16[4,16,32,128]{3,2,1,0:T(8,128)(2,1)S(1)}, u32[]{:S(2)}, u32[]{:S(2)}) collective-permute-start(bf16[4,16,32,128]{3,2,1,0:T(8,128)(2,1)S(1)} %bitcast.127), channel_id=1, source_target_pairs={{0,4},{1,5},{2,6},{3,7},{4,0},{5,1},{6,2},{7,3},{8,12},{9,13},{10,... | collective-permute-start | bytes 1572872 | tf_op jit(solution)/shard_map/ppermute | solution.py:20
  28.6 23.8 %collective-permute-start.3 = (bf16[8,16,32,128]{3,2,0,1:T(8,128)(2,1)S(1)}, bf16[8,16,32,128]{3,2,0,1:T(8,128)(2,1)S(1)}, u32[]{:S(2)}, u32[]{:S(2)}) collective-permute-start(bf16[8,16,32,128]{3,2,0,1:T(8,128)(2,1)S(1)} %copy.19), channel_id=1, source_target_pairs={{0,8},{1,9},{2,10},{3,11},{4,12},{5,13},{6,14},{7,15},{8,0},{9,1},... | collective-permute-start | bytes 3145736 | tf_op jit(solution)/shard_map/ppermute | solution.py:20
  53.1 10.5 %copy-start.7 = (bf16[16,32,128]{2,1,0:T(8,128)(2,1)S(1)}, bf16[16,32,128]{2,1,0:T(8,128)(2,1)}, u32[]{:S(2)}) copy-start(bf16[16,32,128]{2,1,0:T(8,128)(2,1)} %param.9) | copy-start | bytes 393220
  53.8 106.1 %collective-permute-start.4 = (bf16[16,16,32,128]{3,2,0,1:T(8,128)(2,1)S(1)}, bf16[16,16,32,128]{3,2,0,1:T(8,128)(2,1)}, u32[]{:S(2)}, u32[]{:S(2)}) collective-permute-start(bf16[16,16,32,128]{3,2,0,1:T(8,128)(2,1)S(1)} %bitcast.121), channel_id=1, source_target_pairs={{0,16},{1,17},{2,18},{3,19},{4,20},{5,21},{6,22},{7,23},{8,24},{9,... | collective-permute-start | bytes 6291464 | tf_op jit(solution)/shard_map/ppermute | solution.py:20
  59.4 92.3 %all-to-all-start = ((bf16[32,2,2048]{2,1,0:T(2,128)(2,1)}), bf16[32,2,2048]{2,1,0:T(2,128)(2,1)}, u32[]{:S(2)}, u32[]{:S(2)}) async-start(bf16[32,2,2048]{2,1,0:T(2,128)(2,1)} %reshape.64), calls=%async_computation | async-start | bytes 524288 | tf_op jit(solution)/shard_map/all_to_all | solution.py:103
  161.9 3.4 %copy-start.5 = (bf16[128,256]{0,1:T(8,128)(2,1)S(1)}, bf16[128,256]{0,1:T(8,128)(2,1)}, u32[]{:S(2)}) copy-start(bf16[128,256]{0,1:T(8,128)(2,1)} %copy.24) | copy-start | bytes 196612
  165.3 2.1 %copy-start.3 = (bf16[4,32,1024]{2,1,0:T(8,128)(2,1)}, bf16[4,32,1024]{2,1,0:T(8,128)(2,1)S(1)}, u32[]{:S(2)}) copy-start(bf16[4,32,1024]{2,1,0:T(8,128)(2,1)S(1)} %get-tuple-element.262) | copy-start | bytes 786436 | tf_op jit(solution)/shard_map/while
  170.2 1.0 copy-start.2
  174.0 3.5 %copy-start.1 = (f32[16,4,512,32]{2,3,1,0:T(8,128)S(1)}, f32[16,4,512,32]{2,3,1,0:T(8,128)}, u32[]{:S(2)}) copy-start(f32[16,4,512,32]{2,3,1,0:T(8,128)} %get-tuple-element.223) | copy-start | bytes 12582916 | tf_op jit(solution)/shard_map/while
  177.5 1.3 copy-start.4
  177.5 1.3 copy-start.6
  178.8 2.1 %copy-start.3 = (bf16[4,32,1024]{2,1,0:T(8,128)(2,1)}, bf16[4,32,1024]{2,1,0:T(8,128)(2,1)S(1)}, u32[]{:S(2)}) copy-start(bf16[4,32,1024]{2,1,0:T(8,128)(2,1)S(1)} %get-tuple-element.262) | copy-start | bytes 786436 | tf_op jit(solution)/shard_map/while
  183.7 1.0 copy-start.2
  187.5 3.5 %copy-start.1 = (f32[16,4,512,32]{2,3,1,0:T(8,128)S(1)}, f32[16,4,512,32]{2,3,1,0:T(8,128)}, u32[]{:S(2)}) copy-start(f32[16,4,512,32]{2,3,1,0:T(8,128)} %get-tuple-element.223) | copy-start | bytes 12582916 | tf_op jit(solution)/shard_map/while
  191.0 1.3 copy-start.4
  191.0 1.3 copy-start.6
